TPU v7x, 256 devices: a whole 4x4x8 slice. The times are simulated.
256 devices in a mesh: gx: 32 (over x, z_hi, y), vz: 8 (over z_lo, core).
Axes of the slice: x: 4, y: 4, z: 8 (z_hi: 2, z_lo: 4; z = z_hi * 4 + z_lo), core: 2. Of those that a mesh axis runs over, the one named last changes fastest.
Arguments:
- density: float32 [24, 256, 64, 256], P('vz', 'gx'), may hold values from 0.02 to 2.5, as said below
- shift_depth: int32 [16], replicated, may hold values from -20 to 20, as said below
- sub_cell: float32 [16], replicated, may hold values from 0 to 1
- gravity_kick: float32 [256, 64], P('gx'), may hold values from -0.9 to 0.9
- collision: float32 [256, 64], P('gx'), may hold values from 0.1 to 10
Outputs:
- relaxed: float32 [24, 256, 64, 256], P('vz', 'gx')
Inputs may be any that keep to these rules, and one draw needn't show every extreme that they name: `density`: every value is positive. `shift_depth`: some x velocity has 20 and some has -20.
All inputs are finite; a program needn't handle non-finite values.
Results may differ from a plain program's by a relative error of at most 0.00002.
Values sent between devices are 32-bit elements; how exact they have to be, the bound alone decides.
A program may use at most 64 MiB of HBM per device.

v0:
```python
import jax
import jax.numpy as jnp
from jax import lax
from jax.sharding import Mesh
from jax.sharding import PartitionSpec as P

NVX = 16
NVY = 16
VZ = ("vz_0", "vz_1")


def grouped_exchange(x, axis, split_dim, concat_dim, work, item_dim, out_dim):

    def moved(group):
        return lax.all_to_all(group, axis, split_axis=split_dim, concat_axis=concat_dim, tiled=True)

    items = jax.tree.leaves(x)[0].shape[item_dim]
    ends = [items * k // 2 for k in range(2 + 1)] if items % 2 == 0 else [0, items]
    groups = [
        jax.tree.map(lambda a: lax.slice_in_dim(a, low, high, axis=item_dim), x)
        for low, high in zip(ends, ends[1:])
    ]
    arrived = [moved(group) for group in groups]
    made = [work(group) for group in arrived]
    return jax.tree.map(lambda *parts: jnp.concatenate(parts, axis=out_dim), *made)


def padded_2(cells, sides, width):
    for axis, dim in sides:
        count = lax.axis_size(axis)
        ends = count - 1
        head = lax.slice_in_dim(cells, 0, width, axis=dim)
        tail = lax.slice_in_dim(cells, cells.shape[dim] - width, cells.shape[dim], axis=dim)
        cells = jnp.concatenate(
            [
                lax.ppermute(tail, axis, [(i, (i + 1) % count) for i in range(ends)]),
                cells,
                lax.ppermute(head, axis, [((i + 1) % count, i) for i in range(ends)]),
            ],
            axis=dim,
        )
    return cells


def one_axis_at_a_time(x, axes):
    for axis in axes:
        x = lax.psum(x, axis)
    return x


def velocity_values(indices, count, extent):
    return (indices.astype(jnp.float32) - (count - 1) / 2.0) * (extent / count)


def shift_groups(source, starts_near, starts_far, length, sub_cell, axis_x):
    lead = source.shape[:-1]
    grouped = source.reshape(lead + (NVX, NVY))
    pieces = []
    for group in range(NVX):
        column_set = lax.index_in_dim(grouped, group, axis=len(lead), keepdims=False)
        near = lax.dynamic_slice_in_dim(column_set, starts_near[group], length, axis_x)
        far = lax.dynamic_slice_in_dim(column_set, starts_far[group], length, axis_x)
        pieces.append((1.0 - sub_cell[group]) * near + sub_cell[group] * far)
    joined = jnp.stack(pieces, axis=len(lead))
    out_lead = joined.shape[: len(lead)]
    return joined.reshape(out_lead + (NVX * NVY,))


def per_device(density, shift_depth, sub_cell, gravity_kick, collision):
    slab_planes, strip_cols, rows_y, pairs = density.shape
    slab_count = lax.axis_size(VZ)
    total_vz = slab_planes * slab_count
    speed_x = jnp.repeat(velocity_values(jnp.arange(NVX, dtype=jnp.int32), NVX, 9.0), NVY)
    speed_y = jnp.tile(velocity_values(jnp.arange(NVY, dtype=jnp.int32), NVY, 9.0), NVX)
    plane_ids = lax.axis_index(VZ) * slab_planes + jnp.arange(slab_planes, dtype=jnp.int32)
    speed_z = velocity_values(plane_ids, total_vz, 9.6)
    measure_element = 9.0 / NVX * (9.0 / NVY) * (9.6 / total_vz)

    def advect_columns(block):
        width_x = block.shape[1]
        doubled = jnp.concatenate([block, block], axis=1)
        starts_near = jnp.mod(width_x - shift_depth, width_x)
        starts_far = jnp.mod(width_x - shift_depth - 1, width_x)
        shifted = shift_groups(doubled, starts_near, starts_far, width_x, sub_cell, 1)
        return lax.all_to_all(shifted, "gx", split_axis=1, concat_axis=2, tiled=True)

    moved = grouped_exchange(density, "gx", 2, 1, advect_columns, 0, 0)
    padded = padded_2(moved, ((VZ, 0),), 1)
    kick = gravity_kick[None, :, :, None]
    weight_accelerated = (
        (1.0 - jnp.abs(kick)) * moved
        + jnp.maximum(kick, 0.0) * padded[:-2]
        + jnp.maximum(-kick, 0.0) * padded[2:]
    )
    plane_sums = jnp.sum(weight_accelerated, axis=3)
    local_mass = jnp.sum(plane_sums, axis=0)
    local_flow_x = jnp.sum(weight_accelerated * speed_x, axis=(0, 3))
    local_flow_y = jnp.sum(weight_accelerated * speed_y, axis=(0, 3))
    local_flow_z = jnp.sum(plane_sums * speed_z[:, None, None], axis=0)
    energy_terms = speed_x**2 + speed_y**2
    local_energy = jnp.sum(weight_accelerated * energy_terms, axis=(0, 3)) + jnp.sum(
        plane_sums * (speed_z**2)[:, None, None], axis=0
    )
    mass_sum, momentum_x, momentum_y, momentum_z, energy_sum = (
        one_axis_at_a_time(local_mass, VZ),
        one_axis_at_a_time(local_flow_x, VZ),
        one_axis_at_a_time(local_flow_y, VZ),
        one_axis_at_a_time(local_flow_z, VZ),
        one_axis_at_a_time(local_energy, VZ),
    )
    matter_per_cell = measure_element * mass_sum
    flow_x = measure_element * momentum_x / matter_per_cell
    flow_y = measure_element * momentum_y / matter_per_cell
    flow_z = measure_element * momentum_z / matter_per_cell
    speed_sq = flow_x**2 + flow_y**2 + flow_z**2
    motion_warmth = (measure_element * energy_sum - matter_per_cell * speed_sq) / (
        3.0 * matter_per_cell
    )
    deviation_square = (
        (speed_x - flow_x[None, :, :, None]) ** 2
        + (speed_y - flow_y[None, :, :, None]) ** 2
        + (speed_z[:, None, None, None] - flow_z[None, :, :, None]) ** 2
    )
    agitation_width = matter_per_cell * (2.0 * jnp.pi * motion_warmth) ** (-1.5)
    equilibrium_profile = agitation_width[None, :, :, None] * jnp.exp(
        -deviation_square / (2.0 * motion_warmth[None, :, :, None])
    )
    rate = collision[None, :, :, None]
    return (weight_accelerated + rate * equilibrium_profile) / (1.0 + rate)


def solution(mesh):
    torus = Mesh(mesh.devices.reshape(mesh.shape["gx"], 4, 2), ("gx", "vz_0", "vz_1"))
    return jax.shard_map(
        per_device,
        mesh=torus,
        in_specs=(P(VZ, "gx", None, None), P(), P(), P("gx", None), P("gx", None)),
        out_specs=P(VZ, "gx", None, None),
        check_vma=False,
    )
```

profile of v0, /device:TPU:1, one launch (start us, length us, event | category | flops | bytes accessed | tf_op | source)
XLA Modules:
  0.0 214.6 jit_solution(9858659908536691685)
XLA Ops:
  0.0 3.5 %copy.57 = f32[3,8,64,256]{3,1,0,2:T(8,128)} copy(f32[3,8,64,256]{3,2,1,0:T(8,128)} %param.5) | data formatting | bytes 3145728 | tf_op args[0]
  3.5 14.6 %all-to-all-start = ((f32[3,8,64,256]{3,1,0,2:T(8,128)}), f32[3,8,64,256]{3,1,0,2:T(8,128)S(1)}, u32[]{:S(2)}, u32[]{:S(2)}) async-start(f32[3,8,64,256]{3,1,0,2:T(8,128)} %copy.57), calls=%async_computation | async-start | bytes 3145728 | tf_op jit(solution)/shard_map/all_to_all | solution.py:15
  18.1 0.7 fusion.29
  20.1 0.7 fusion.28
  59.7 0.7 fusion.27
  90.3 0.1 copy.85
  90.4 6.6 %concatenate.13 = f32[3,256,2,16,16]{4,3,1,2,0:T(8,128)} reshape(f32[3,32,8,2,256]{4,2,1,3,0:T(8,128)S(1)} %bitcast.69) | data formatting | bytes 3145728 | tf_op jit(solution)/shard_map/concatenate | solution.py:81
  97.1 8.9 %copy.59 = f32[3,256,2,16,16]{1,4,3,2,0:T(8,128)S(1)} copy(f32[3,256,2,16,16]{4,3,1,2,0:T(8,128)} %concatenate.13) | data formatting | bytes 3145728 | tf_op jit(solution)/shard_map/concatenate | solution.py:81
  106.0 0.1 fusion.18
  106.1 0.1 fusion.4
  106.2 0.7 add_dynamic-update-slice_fusion.14
  107.0 0.8 add_dynamic-update-slice_fusion.13
  107.7 0.7 add_dynamic-update-slice_fusion.12
  108.5 0.7 add_dynamic-update-slice_fusion.11
  109.2 0.8 add_dynamic-update-slice_fusion.10
  109.9 0.7 add_dynamic-update-slice_fusion.9
  110.6 0.8 add_dynamic-update-slice_fusion.8
  111.3 0.8 add_dynamic-update-slice_fusion.7
  112.1 0.7 add_dynamic-update-slice_fusion.6
  112.8 0.7 add_dynamic-update-slice_fusion.5
  113.6 0.7 add_dynamic-update-slice_fusion.4
  114.3 0.8 add_dynamic-update-slice_fusion.3
  115.1 0.7 add_dynamic-update-slice_fusion.2
  115.9 0.8 add_dynamic-update-slice_fusion.1
  116.7 0.7 add_dynamic-update-slice_fusion
  117.4 0.8 fusion.21
  118.2 2.1 copy.61
  120.3 11.8 %all-to-all-start.1 = ((f32[3,256,2,256]{3,2,0,1:T(2,128)}), f32[3,256,2,256]{3,2,0,1:T(2,128)S(1)}, u32[]{:S(2)}, u32[]{:S(2)}) async-start(f32[3,256,2,256]{3,2,0,1:T(2,128)} %copy.61), calls=%async_computation.1 | async-start | bytes 3145728 | tf_op jit(solution)/shard_map/all_to_all | solution.py:85
  132.1 0.1 tile.18
  132.2 0.1 broadcast_in_dim.6
  132.3 0.1 reshape.131
  132.3 0.1 copy.66
  132.4 0.1 copy.64
  132.5 0.1 copy.56
  132.6 0.1 copy.68
  132.7 27.6 %all-to-all-done.1 = f32[3,256,2,256]{3,2,0,1:T(2,128)S(1)} async-done(((f32[3,256,2,256]{3,2,0,1:T(2,128)}), f32[3,256,2,256]{3,2,0,1:T(2,128)S(1)}, u32[]{:S(2)}, u32[]{:S(2)}) %all-to-all-start.1) | async-done | bytes 1572896 | tf_op jit(solution)/shard_map/all_to_all | solution.py:85
  160.2 0.1 copy.84
  160.4 0.1 fusion.26
  160.5 16.7 %collective-permute-start.1 = (f32[1,8,64,256]{3,1,2,0:T(8,128)S(1)}, f32[1,8,64,256]{3,1,2,0:T(8,128)S(1)}, u32[]{:S(2)}, u32[]{:S(2)}) collective-permute-start(f32[1,8,64,256]{3,1,2,0:T(8,128)S(1)} %bitcast.71), channel_id=1, source_target_pairs={{1,0},{2,1},{3,2},{4,3},{5,4},{6,5},{7,6},{9,8},{10,9},{11,10},{12... | collective-permute-start | bytes 1572872 | tf_op jit(solution)/shard_map/ppermute | solution.py:38
  177.2 0.9 copy.65
  178.1 3.2 %collective-permute-start = (f32[1,8,64,256]{3,1,2,0:T(8,128)}, f32[1,8,64,256]{3,1,2,0:T(8,128)S(1)}, u32[]{:S(2)}, u32[]{:S(2)}) collective-permute-start(f32[1,8,64,256]{3,1,2,0:T(8,128)} %bitcast.55), channel_id=1, source_target_pairs={{0,1},{1,2},{2,3},{3,4},{4,5},{5,6},{6,7},{8,9},{9,10},{10,11},{11... | collective-permute-start | bytes 1572872 | tf_op jit(solution)/shard_map/ppermute | solution.py:36
  181.3 0.1 copy.80
  181.4 0.2 copy.63
  181.6 3.8 %collective-permute-done.1 = f32[1,8,64,256]{3,1,2,0:T(8,128)S(1)} collective-permute-done((f32[1,8,64,256]{3,1,2,0:T(8,128)S(1)}, f32[1,8,64,256]{3,1,2,0:T(8,128)S(1)}, u32[]{:S(2)}, u32[]{:S(2)}) %collective-permute-start.1) | collective-permute-done | bytes 524320 | tf_op jit(solution)/shard_map/ppermute | solution.py:38
  185.4 2.3 %collective-permute-done = f32[1,8,64,256]{3,1,2,0:T(8,128)S(1)} collective-permute-done((f32[1,8,64,256]{3,1,2,0:T(8,128)}, f32[1,8,64,256]{3,1,2,0:T(8,128)S(1)}, u32[]{:S(2)}, u32[]{:S(2)}) %collective-permute-start) | collective-permute-done | bytes 524320 | tf_op jit(solution)/shard_map/ppermute | solution.py:36
  187.7 1.4 multiply_reduce_fusion
  189.1 0.1 copy.69
  189.2 0.1 copy.70
  189.2 0.1 multiply_reduce_fusion.3
  189.3 0.1 copy.71
  189.4 0.1 copy.72
  189.5 0.1 copy.73
  189.5 0.1 copy.74
  189.6 12.9 %all-reduce = (f32[8,64]{1,0:T(8,128)S(1)}, f32[8,64]{1,0:T(8,128)S(1)}, f32[8,64]{1,0:T(8,128)S(1)}, f32[8,64]{1,0:T(8,128)S(1)}, f32[8,64]{1,0:T(8,128)S(1)}) all-reduce(f32[8,64]{1,0:T(8,128)S(1)} %copy.69, f32[8,64]{1,0:T(8,128)S(1)} %add.335, f32[8,64]{1,0:T(8,128)S(1)} %copy.72, ...), channel_id=1, replica_groups=mesh['gx'=32,'vz_0'=4,'vz_1'=2] {'vz_0'}, use_global_device_ids=true, to_apply=%region_1.2 | all-reduce | flops 2560 | bytes 20480 | tf_op jit(solution)/shard_map/psum | solution.py:47
  202.5 9.0 %all-reduce.1 = (f32[8,64]{1,0:T(8,128)S(1)}, f32[8,64]{1,0:T(8,128)S(1)}, f32[8,64]{1,0:T(8,128)S(1)}, f32[8,64]{1,0:T(8,128)S(1)}, f32[8,64]{1,0:T(8,128)S(1)}) all-reduce(f32[8,64]{1,0:T(8,128)S(1)} %get-tuple-element.12, f32[8,64]{1,0:T(8,128)S(1)} %get-tuple-element.13, ...), channel_id=1, replica_groups=mesh['gx'=32,'vz_0'=4,'vz_1'=2] {'vz_1'}, use_global_device_ids=true, to_apply=%region_2.3 | all-reduce | flops 2560 | bytes 20480 | tf_op jit(solution)/shard_map/psum | solution.py:47
  211.5 0.1 copy.79
  211.6 0.1 copy.78
  211.7 0.1 subtract_multiply_fusion
  211.8 0.1 copy.77
  211.9 0.1 copy.76
  211.9 0.1 copy.75
  212.0 0.2 multiply_add_fusion
  212.2 0.7 add_divide_fusion
  212.9 1.6 copy.81
  (20 shorter events, 0.1 us)
Async XLA Ops:
  3.5 14.6 %copy-start.3 = (s32[16]{0:T(128)S(1)}, s32[16]{0:T(128)}, u32[]{:S(2)}) copy-start(s32[16]{0:T(128)} %param.6) | copy-start | bytes 196
  3.5 56.2 %copy-start = (f32[16]{0:T(128)S(1)}, f32[16]{0:T(128)}, u32[]{:S(2)}) copy-start(f32[16]{0:T(128)} %param.7) | copy-start | bytes 196
  3.5 86.8 %all-to-all-start = ((f32[3,8,64,256]{3,1,0,2:T(8,128)}), f32[3,8,64,256]{3,1,0,2:T(8,128)S(1)}, u32[]{:S(2)}, u32[]{:S(2)}) async-start(f32[3,8,64,256]{3,1,0,2:T(8,128)} %copy.57), calls=%async_computation | async-start | bytes 3145728 | tf_op jit(solution)/shard_map/all_to_all | solution.py:15
  120.3 12.0 %copy-start.2 = (f32[8,64]{1,0:T(8,128)S(1)}, f32[8,64]{1,0:T(8,128)}, u32[]{:S(2)}) copy-start(f32[8,64]{1,0:T(8,128)} %param.8) | copy-start | bytes 6148
  120.3 12.3 %copy-start.1 = (f32[8,64]{1,0:T(8,128)S(1)}, f32[8,64]{1,0:T(8,128)}, u32[]{:S(2)}) copy-start(f32[8,64]{1,0:T(8,128)} %param.9) | copy-start | bytes 6148
  120.3 39.9 %all-to-all-start.1 = ((f32[3,256,2,256]{3,2,0,1:T(2,128)}), f32[3,256,2,256]{3,2,0,1:T(2,128)S(1)}, u32[]{:S(2)}, u32[]{:S(2)}) async-start(f32[3,256,2,256]{3,2,0,1:T(2,128)} %copy.61), calls=%async_computation.1 | async-start | bytes 3145728 | tf_op jit(solution)/shard_map/all_to_all | solution.py:85
  160.5 24.9 %collective-permute-start.1 = (f32[1,8,64,256]{3,1,2,0:T(8,128)S(1)}, f32[1,8,64,256]{3,1,2,0:T(8,128)S(1)}, u32[]{:S(2)}, u32[]{:S(2)}) collective-permute-start(f32[1,8,64,256]{3,1,2,0:T(8,128)S(1)} %bitcast.71), channel_id=1, source_target_pairs={{1,0},{2,1},{3,2},{4,3},{5,4},{6,5},{7,6},{9,8},{10,9},{11,10},{12... | collective-permute-start | bytes 1572872 | tf_op jit(solution)/shard_map/ppermute | solution.py:38
  178.1 9.7 %collective-permute-start = (f32[1,8,64,256]{3,1,2,0:T(8,128)}, f32[1,8,64,256]{3,1,2,0:T(8,128)S(1)}, u32[]{:S(2)}, u32[]{:S(2)}) collective-permute-start(f32[1,8,64,256]{3,1,2,0:T(8,128)} %bitcast.55), channel_id=1, source_target_pairs={{0,1},{1,2},{2,3},{3,4},{4,5},{5,6},{6,7},{8,9},{9,10},{10,11},{11... | collective-permute-start | bytes 1572872 | tf_op jit(solution)/shard_map/ppermute | solution.py:36
where the time goes:
time: 216 us; the launch traced here: 215 us
  between operations  70.4 us (33%)
  starting transfers between devices  46.3 us (21%)
  waiting for transfers between devices  33.7 us (16%)
  local copies, waits for them, and re-layouts  27.8 us (13%)
  blocking collectives  21.9 us (10%)
  other arithmetic  14.6 us (7%)
    all_to_all x1, waiting for transfers between devices, advect_columns(): lax.all_to_all(shifted, 'gx', split_axis=1, concat_axis=2, tiled=True)  27.6 us
    psum x2, blocking collectives, one_axis_at_a_time(): x = lax.psum(x, axis)  21.9 us
    ppermute x1, starting transfers between devices, padded_2(): lax.ppermute(head, axis, [((i + 1) % count, i) for i in range(ends)])  16.7 us
    concatenate x2, local copies, waits for them, and re-layouts, advect_columns(): doubled = jnp.concatenate([block, block], axis=1)  15.6 us
    all_to_all x1, starting transfers between devices, moved(): lax.all_to_all(group, axis, split_axis=split_dim, concat_axis=concat_dim,...  14.6 us
    all_to_all x1, starting transfers between devices, advect_columns(): lax.all_to_all(shifted, 'gx', split_axis=1, concat_axis=2, tiled=True)  11.8 us
    unnamed x15, other arithmetic  11.1 us
  transfers between devices with their start and end apart: 4, of which 3 were waited for; matrix products, arithmetic and copies ran while one was open for 2% of the time, Pallas kernels for 0%

commit v1 on v0

--- a/solution.py
+++ b/solution.py
@@ -44,7 +44,7 @@
 
 def one_axis_at_a_time(x, axes):
     for axis in axes:
-        x = lax.psum(x, axis)
+        x = jnp.sum(jax.lax.all_gather(x, axis_name=axis), axis=0)
     return x
 
 

time: 216 us -> 270 us (1.25)
  blocking collectives: 21.9 us -> 75.6 us
    all_gather x0 -> x10, blocking collectives: none -> 75.6 us  [one_axis_at_a_time(): x = jnp.sum(jax.lax.all_gather(x, axis_name=axis), axis=0)]
    psum x2 -> x0, blocking collectives: 21.9 us -> none  [one_axis_at_a_time(): x = lax.psum(x, axis)]
  transfers between devices with their start and end apart: 4 -> 4, of which waited for: 3 -> 3; matrix products, arithmetic and copies ran while one was open for 2% -> 1% of each run, Pallas kernels for 0% -> 0%
where the time goes in v1:
time: 270 us; the launch traced here: 268 us
  blocking collectives  75.6 us (28%)
  between operations  70.4 us (26%)
  starting transfers between devices  46.3 us (17%)
  waiting for transfers between devices  33.7 us (12%)
  local copies, waits for them, and re-layouts  27.7 us (10%)
  other arithmetic  14.6 us (5%)
    all_gather x10, blocking collectives, one_axis_at_a_time(): x = jnp.sum(jax.lax.all_gather(x, axis_name=axis), axis=0)  75.6 us
    all_to_all x1, waiting for transfers between devices, advect_columns(): lax.all_to_all(shifted, 'gx', split_axis=1, concat_axis=2, tiled=True)  27.6 us
    ppermute x1, starting transfers between devices, padded_2(): lax.ppermute(head, axis, [((i + 1) % count, i) for i in range(ends)])  16.7 us
    concatenate x2, local copies, waits for them, and re-layouts, advect_columns(): doubled = jnp.concatenate([block, block], axis=1)  15.6 us
    all_to_all x1, starting transfers between devices, moved(): lax.all_to_all(group, axis, split_axis=split_dim, concat_axis=concat_dim,...  14.6 us
    all_to_all x1, starting transfers between devices, advect_columns(): lax.all_to_all(shifted, 'gx', split_axis=1, concat_axis=2, tiled=True)  11.8 us
    unnamed x15, other arithmetic  11.1 us
  transfers between devices with their start and end apart: 4, of which 3 were waited for; matrix products, arithmetic and copies ran while one was open for 1% of the time, Pallas kernels for 0%

profile of v1, /device:TPU:1, one launch (start us, length us, event | category | flops | bytes accessed | tf_op | source)
XLA Modules:
  0.0 268.3 jit_solution(3271098140578557144)
XLA Ops:
  0.0 3.5 %copy.77 = f32[3,8,64,256]{3,1,0,2:T(8,128)} copy(f32[3,8,64,256]{3,2,1,0:T(8,128)} %param.5) | data formatting | bytes 3145728 | tf_op args[0]
  3.5 14.6 %all-to-all-start = ((f32[3,8,64,256]{3,1,0,2:T(8,128)}), f32[3,8,64,256]{3,1,0,2:T(8,128)S(1)}, u32[]{:S(2)}, u32[]{:S(2)}) async-start(f32[3,8,64,256]{3,1,0,2:T(8,128)} %copy.77), calls=%async_computation | async-start | bytes 3145728 | tf_op jit(solution)/shard_map/all_to_all | solution.py:15
  18.1 0.7 fusion.29
  20.1 0.7 fusion.28
  59.7 0.7 fusion.27
  90.3 0.1 copy.104
  90.4 6.6 %concatenate.13 = f32[3,256,2,16,16]{4,3,1,2,0:T(8,128)} reshape(f32[3,32,8,2,256]{4,2,1,3,0:T(8,128)S(1)} %bitcast.89) | data formatting | bytes 3145728 | tf_op jit(solution)/shard_map/concatenate | solution.py:81
  97.1 8.9 %copy.79 = f32[3,256,2,16,16]{1,4,3,2,0:T(8,128)S(1)} copy(f32[3,256,2,16,16]{4,3,1,2,0:T(8,128)} %concatenate.13) | data formatting | bytes 3145728 | tf_op jit(solution)/shard_map/concatenate | solution.py:81
  106.0 0.1 fusion.18
  106.1 0.1 fusion.4
  106.2 0.7 add_dynamic-update-slice_fusion.14
  107.0 0.8 add_dynamic-update-slice_fusion.13
  107.7 0.7 add_dynamic-update-slice_fusion.12
  108.5 0.7 add_dynamic-update-slice_fusion.11
  109.2 0.8 add_dynamic-update-slice_fusion.10
  109.9 0.7 add_dynamic-update-slice_fusion.9
  110.6 0.8 add_dynamic-update-slice_fusion.8
  111.3 0.8 add_dynamic-update-slice_fusion.7
  112.1 0.7 add_dynamic-update-slice_fusion.6
  112.8 0.7 add_dynamic-update-slice_fusion.5
  113.6 0.7 add_dynamic-update-slice_fusion.4
  114.3 0.8 add_dynamic-update-slice_fusion.3
  115.1 0.7 add_dynamic-update-slice_fusion.2
  115.9 0.8 add_dynamic-update-slice_fusion.1
  116.7 0.7 add_dynamic-update-slice_fusion
  117.4 0.8 fusion.21
  118.2 2.1 copy.81
  120.3 11.8 %all-to-all-start.1 = ((f32[3,256,2,256]{3,2,0,1:T(2,128)}), f32[3,256,2,256]{3,2,0,1:T(2,128)S(1)}, u32[]{:S(2)}, u32[]{:S(2)}) async-start(f32[3,256,2,256]{3,2,0,1:T(2,128)} %copy.81), calls=%async_computation.1 | async-start | bytes 3145728 | tf_op jit(solution)/shard_map/all_to_all | solution.py:85
  132.1 0.1 tile.18
  132.3 0.1 reshape.191
  132.3 0.1 copy.86
  132.4 0.1 copy.84
  132.5 0.1 copy.76
  132.6 0.1 copy.88
  132.7 27.6 %all-to-all-done.1 = f32[3,256,2,256]{3,2,0,1:T(2,128)S(1)} async-done(((f32[3,256,2,256]{3,2,0,1:T(2,128)}), f32[3,256,2,256]{3,2,0,1:T(2,128)S(1)}, u32[]{:S(2)}, u32[]{:S(2)}) %all-to-all-start.1) | async-done | bytes 1572896 | tf_op jit(solution)/shard_map/all_to_all | solution.py:85
  160.2 0.1 copy.103
  160.5 16.7 %collective-permute-start.1 = (f32[1,8,64,256]{3,1,2,0:T(8,128)S(1)}, f32[1,8,64,256]{3,1,2,0:T(8,128)S(1)}, u32[]{:S(2)}, u32[]{:S(2)}) collective-permute-start(f32[1,8,64,256]{3,1,2,0:T(8,128)S(1)} %bitcast.91), channel_id=1, source_target_pairs={{1,0},{2,1},{3,2},{4,3},{5,4},{6,5},{7,6},{9,8},{10,9},{11,10},{12... | collective-permute-start | bytes 1572872 | tf_op jit(solution)/shard_map/ppermute | solution.py:38
  177.2 0.9 copy.85
  178.1 3.2 %collective-permute-start = (f32[1,8,64,256]{3,1,2,0:T(8,128)}, f32[1,8,64,256]{3,1,2,0:T(8,128)S(1)}, u32[]{:S(2)}, u32[]{:S(2)}) collective-permute-start(f32[1,8,64,256]{3,1,2,0:T(8,128)} %bitcast.55), channel_id=1, source_target_pairs={{0,1},{1,2},{2,3},{3,4},{4,5},{5,6},{6,7},{8,9},{9,10},{10,11},{11... | collective-permute-start | bytes 1572872 | tf_op jit(solution)/shard_map/ppermute | solution.py:36
  181.3 0.1 copy.99
  181.4 0.2 copy.83
  181.6 3.8 %collective-permute-done.1 = f32[1,8,64,256]{3,1,2,0:T(8,128)S(1)} collective-permute-done((f32[1,8,64,256]{3,1,2,0:T(8,128)S(1)}, f32[1,8,64,256]{3,1,2,0:T(8,128)S(1)}, u32[]{:S(2)}, u32[]{:S(2)}) %collective-permute-start.1) | collective-permute-done | bytes 524320 | tf_op jit(solution)/shard_map/ppermute | solution.py:38
  185.4 2.3 collective-permute-done
  187.7 1.4 multiply_reduce_fusion
  189.2 10.3 %all-gather = f32[32,64]{1,0:T(8,128)S(1)} all-gather(f32[8,64]{1,0:T(8,128)S(1)} %copy.89), channel_id=2, replica_groups=mesh['gx'=32,'vz_0'=4,'vz_1'=2] {'vz_0'}, dimensions={0}, use_global_device_ids=true | all-gather | bytes 10240 | tf_op jit(solution)/shard_map/all_gather | solution.py:47
  199.5 5.2 %all-gather.1 = f32[16,64]{1,0:T(8,128)S(1)} all-gather(f32[8,64]{1,0:T(8,128)S(1)} %bitcast_reduce_fusion.4), channel_id=3, replica_groups=mesh['gx'=32,'vz_0'=4,'vz_1'=2] {'vz_1'}, dimensions={0}, use_global_device_ids=true | all-gather | bytes 6144 | tf_op jit(solution)/shard_map/all_gather | solution.py:47
  204.7 0.1 multiply_reduce_fusion.3
  204.9 10.3 %all-gather.8 = f32[32,64]{1,0:T(8,128)S(1)} all-gather(f32[8,64]{1,0:T(8,128)S(1)} %copy.93), channel_id=10, replica_groups=mesh['gx'=32,'vz_0'=4,'vz_1'=2] {'vz_0'}, dimensions={0}, use_global_device_ids=true | all-gather | bytes 10240 | tf_op jit(solution)/shard_map/all_gather | solution.py:47
  215.2 4.7 %all-gather.9 = f32[16,64]{1,0:T(8,128)S(1)} all-gather(f32[8,64]{1,0:T(8,128)S(1)} %bitcast_reduce_fusion), channel_id=11, replica_groups=mesh['gx'=32,'vz_0'=4,'vz_1'=2] {'vz_1'}, dimensions={0}, use_global_device_ids=true | all-gather | bytes 6144 | tf_op jit(solution)/shard_map/all_gather | solution.py:47
  220.0 10.3 %all-gather.6 = f32[32,64]{1,0:T(8,128)S(1)} all-gather(f32[8,64]{1,0:T(8,128)S(1)} %copy.92), channel_id=8, replica_groups=mesh['gx'=32,'vz_0'=4,'vz_1'=2] {'vz_0'}, dimensions={0}, use_global_device_ids=true | all-gather | bytes 10240 | tf_op jit(solution)/shard_map/all_gather | solution.py:47
  230.3 4.7 %all-gather.7 = f32[16,64]{1,0:T(8,128)S(1)} all-gather(f32[8,64]{1,0:T(8,128)S(1)} %bitcast_reduce_fusion.1), channel_id=9, replica_groups=mesh['gx'=32,'vz_0'=4,'vz_1'=2] {'vz_1'}, dimensions={0}, use_global_device_ids=true | all-gather | bytes 6144 | tf_op jit(solution)/shard_map/all_gather | solution.py:47
  235.1 10.3 %all-gather.4 = f32[32,64]{1,0:T(8,128)S(1)} all-gather(f32[8,64]{1,0:T(8,128)S(1)} %copy.91), channel_id=6, replica_groups=mesh['gx'=32,'vz_0'=4,'vz_1'=2] {'vz_0'}, dimensions={0}, use_global_device_ids=true | all-gather | bytes 10240 | tf_op jit(solution)/shard_map/all_gather | solution.py:47
  245.4 4.7 %all-gather.5 = f32[16,64]{1,0:T(8,128)S(1)} all-gather(f32[8,64]{1,0:T(8,128)S(1)} %bitcast_reduce_fusion.2), channel_id=7, replica_groups=mesh['gx'=32,'vz_0'=4,'vz_1'=2] {'vz_1'}, dimensions={0}, use_global_device_ids=true | all-gather | bytes 6144 | tf_op jit(solution)/shard_map/all_gather | solution.py:47
  250.2 10.3 %all-gather.2 = f32[32,64]{1,0:T(8,128)S(1)} all-gather(f32[8,64]{1,0:T(8,128)S(1)} %copy.90), channel_id=4, replica_groups=mesh['gx'=32,'vz_0'=4,'vz_1'=2] {'vz_0'}, dimensions={0}, use_global_device_ids=true | all-gather | bytes 10240 | tf_op jit(solution)/shard_map/all_gather | solution.py:47
  260.5 4.7 %all-gather.3 = f32[16,64]{1,0:T(8,128)S(1)} all-gather(f32[8,64]{1,0:T(8,128)S(1)} %bitcast_reduce_fusion.3), channel_id=5, replica_groups=mesh['gx'=32,'vz_0'=4,'vz_1'=2] {'vz_1'}, dimensions={0}, use_global_device_ids=true | all-gather | bytes 6144 | tf_op jit(solution)/shard_map/all_gather | solution.py:47
  265.2 0.1 copy.98
  265.3 0.1 copy.97
  265.4 0.1 subtract_multiply_fusion
  265.5 0.1 copy.96
  265.6 0.1 copy.95
  265.7 0.1 copy.94
  265.7 0.2 multiply_add_fusion
  266.0 0.7 add_divide_fusion
  266.6 1.6 copy.100
  (37 shorter events, 0.6 us)
Async XLA Ops:
  3.5 14.6 %copy-start.3 = (s32[16]{0:T(128)S(1)}, s32[16]{0:T(128)}, u32[]{:S(2)}) copy-start(s32[16]{0:T(128)} %param.6) | copy-start | bytes 196
  3.5 56.2 %copy-start = (f32[16]{0:T(128)S(1)}, f32[16]{0:T(128)}, u32[]{:S(2)}) copy-start(f32[16]{0:T(128)} %param.7) | copy-start | bytes 196
  3.5 86.8 %all-to-all-start = ((f32[3,8,64,256]{3,1,0,2:T(8,128)}), f32[3,8,64,256]{3,1,0,2:T(8,128)S(1)}, u32[]{:S(2)}, u32[]{:S(2)}) async-start(f32[3,8,64,256]{3,1,0,2:T(8,128)} %copy.77), calls=%async_computation | async-start | bytes 3145728 | tf_op jit(solution)/shard_map/all_to_all | solution.py:15
  120.3 12.0 %copy-start.2 = (f32[8,64]{1,0:T(8,128)S(1)}, f32[8,64]{1,0:T(8,128)}, u32[]{:S(2)}) copy-start(f32[8,64]{1,0:T(8,128)} %param.8) | copy-start | bytes 6148
  120.3 12.3 %copy-start.1 = (f32[8,64]{1,0:T(8,128)S(1)}, f32[8,64]{1,0:T(8,128)}, u32[]{:S(2)}) copy-start(f32[8,64]{1,0:T(8,128)} %param.9) | copy-start | bytes 6148
  120.3 39.9 %all-to-all-start.1 = ((f32[3,256,2,256]{3,2,0,1:T(2,128)}), f32[3,256,2,256]{3,2,0,1:T(2,128)S(1)}, u32[]{:S(2)}, u32[]{:S(2)}) async-start(f32[3,256,2,256]{3,2,0,1:T(2,128)} %copy.81), calls=%async_computation.1 | async-start | bytes 3145728 | tf_op jit(solution)/shard_map/all_to_all | solution.py:85
  160.5 24.9 %collective-permute-start.1 = (f32[1,8,64,256]{3,1,2,0:T(8,128)S(1)}, f32[1,8,64,256]{3,1,2,0:T(8,128)S(1)}, u32[]{:S(2)}, u32[]{:S(2)}) collective-permute-start(f32[1,8,64,256]{3,1,2,0:T(8,128)S(1)} %bitcast.91), channel_id=1, source_target_pairs={{1,0},{2,1},{3,2},{4,3},{5,4},{6,5},{7,6},{9,8},{10,9},{11,10},{12... | collective-permute-start | bytes 1572872 | tf_op jit(solution)/shard_map/ppermute | solution.py:38
  178.1 9.7 %collective-permute-start = (f32[1,8,64,256]{3,1,2,0:T(8,128)}, f32[1,8,64,256]{3,1,2,0:T(8,128)S(1)}, u32[]{:S(2)}, u32[]{:S(2)}) collective-permute-start(f32[1,8,64,256]{3,1,2,0:T(8,128)} %bitcast.55), channel_id=1, source_target_pairs={{0,1},{1,2},{2,3},{3,4},{4,5},{5,6},{6,7},{8,9},{9,10},{10,11},{11... | collective-permute-start | bytes 1572872 | tf_op jit(solution)/shard_map/ppermute | solution.py:36
